TPU v7x, 256 devices: a whole 4x4x8 slice. The times are simulated.
256 devices in a mesh: gx: 4 (over x), gy: 8 (over z), gz: 8 (over y, core).
Axes of the slice: x: 4, y: 4, z: 8, core: 2. Of those that a mesh axis runs over, the one named last changes fastest.
Arguments:
- conduct: float32 [3, 128, 128, 512], P(None, 'gz', 'gy', 'gx'), may hold values from 0.5 to 2
- cross: float32 [3, 128, 128, 512], P(None, 'gz', 'gy', 'gx'), may hold values from -0.25 to 0.25
- tissue: int32 [128, 128, 512], P('gz', 'gy', 'gx'), may hold values 0 or 1
- src_z: int32 [2048], replicated, may hold values from 0 to 127
- src_y: int32 [2048], replicated, may hold values from 0 to 127
- src_x: int32 [2048], replicated, may hold values from 0 to 511
Outputs:
- solution: float32 [128, 128, 512], P('gz', 'gy', 'gx')
All inputs are finite; a program needn't handle non-finite values. No bound on the sum of `tissue` on one device may be relied on, other than what follows from the above.
Results may differ from a plain program's by a relative error of at most 0.0001.
Values sent between devices are 32-bit elements; how exact they have to be, the bound alone decides.
A program may use at most 128 MiB of HBM per device.

v0:
```python
import functools

import jax
import jax.numpy as jnp
from jax import lax
from jax.experimental import pallas as pl
from jax.experimental.pallas import tpu as pltpu
from jax.sharding import PartitionSpec as P

tau_step = 4000.0
relax = 0.55
stim_height = 64000.0
COARSE = 12
RO = 8
LANES = 128
MESH = pl.DeviceIdType.MESH
F32 = jnp.float32
PAIRS = ((0, 1, 3), (0, 2, 4), (1, 2, 5))


class Level:
    def __init__(self, index, nz, ny, nx, split):
        self.index, self.nz, self.ny, self.nx, self.split = index, nz, ny, nx, split
        self.rows = max(8, -(-ny // 8) * 8)
        self.zrows = max(8, -(-nz // 8) * 8)
        self.stride = RO + self.rows + 8
        self.tau = tau_step / 4.0**index
        self.right = nx % LANES


def lanes_of(shape):
    return lax.broadcasted_iota(jnp.int32, shape, len(shape) - 1)


def rows_of(shape):
    return lax.broadcasted_iota(jnp.int32, shape, len(shape) - 2)


def roll(value, shift, axis=None):
    axis = value.ndim - 1 if axis is None else axis
    if isinstance(shift, int):
        shift = shift % value.shape[axis]
        if shift == 0:
            return value
    return pltpu.roll(value, shift, axis)


def dot(a, b):
    return lax.dot_general(
        a, b, (((1,), (0,)), ((), ())), precision=lax.Precision.HIGHEST, preferred_element_type=F32
    )


MESSAGES = [("z", 1, (0, 0, -1)), ("z", 0, (0, 0, 1))]
for _face, _oy in ((0, -1), (1, 1)):
    for _part, _oz in ((0, 0), (1, -1), (2, 1)):
        MESSAGES.append(("y", 3 * _face + _part, (0, _oy, _oz)))
for _side, _ox in ((0, -1), (1, 1)):
    for _part, (_oy, _oz) in enumerate(((0, 0), (-1, 0), (1, 0), (0, -1), (0, 1))):
        MESSAGES.append(("p", 5 * _side + _part, (_ox, _oy, _oz)))
FACES = [("z", 1, (0, 0, -1)), ("z", 0, (0, 0, 1)), ("y", 0, (0, -1, 0)), ("y", 1, (0, 1, 0)), ("p", 0, (-1, 0, 0)), ("p", 1, (1, 0, 0))]


def kernel(names, levels, sizes, sources, *refs):
    R = dict(zip(names, refs))
    GX, GY, GZ = sizes
    gx, gy, gz = lax.axis_index("gx"), lax.axis_index("gy"), lax.axis_index("gz")

    def device(ox, oy, oz):
        return (lax.rem(gx + (ox + GX), GX), lax.rem(gy + (oy + GY), GY), lax.rem(gz + (oz + GZ), GZ))

    peers = [offset for _, _, offset in MESSAGES]
    peers += [(k, 0, 0) for k in range(1, GX)] + [(0, k, 0) for k in range(1, GY)] + [(0, 0, k) for k in range(1, GZ)]
    seen, unique = set(), []
    for ox, oy, oz in peers:
        key = (ox % GX, oy % GY, oz % GZ)
        if key not in seen:
            seen.add(key)
            unique.append(key)
    barrier = pltpu.get_barrier_semaphore()
    for ox, oy, oz in unique:
        pl.semaphore_signal(barrier, inc=1, device_id=device(ox, oy, oz), device_id_type=MESH)

    def flag(condition):
        return jnp.where(condition, 0.0, 1.0).astype(F32)

    in_xp, in_xm = flag(gx == GX - 1), flag(gx == 0)
    in_yp, in_ym = flag(gy == GY - 1), flag(gy == 0)
    in_zp, in_zm = flag(gz == GZ - 1), flag(gz == 0)

    def clean(level, value):
        return value if level.ny == level.rows else jnp.where(rows_of(value.shape) < level.ny, value, 0.0)

    def bounds(level):
        if level.split:
            return in_zp, in_zm, in_yp, in_ym, in_xp, in_xm
        return (jnp.zeros((), F32),) * 6

    def pack_x(level, get):
        shape = (level.rows, LANES)
        lane = lanes_of(shape)
        out = jnp.zeros(shape, F32)
        for z in range(level.nz):
            value = get(z)
            first = (level.right + 2 * (z + 1)) % LANES
            last = (2 * (z + 1) + LANES - 1) % LANES
            a = roll(value, first)
            b = roll(value, last - (level.nx - 1))
            out = jnp.where(lane == first, a, jnp.where(lane == last, b, out))
        return out

    def coarsen_rows(level, lower, get, count):
        stage = R["stage"]
        half = level.ny // 2
        for i in range(count):
            for z in range(level.nz // 2):
                total = None
                for dz in range(2):
                    for dy in range(2):
                        piece = get(i, 2 * z + dz, pl.ds(RO + dy, half, stride=2))
                        total = piece if total is None else total + piece
                stage[pl.ds((i * (level.nz // 2) + z) * lower.rows, half), :] = total

    def coarsen_lanes(level, rows):
        a, b = rows_of((LANES, LANES)), lanes_of((LANES, LANES))
        matrix = jnp.where((b == a // 2) & (b < level.nx // 2), 0.125, 0.0).astype(F32)
        return dot(R["stage"][pl.ds(0, rows), :], matrix)

    def coefficients(level):
        l = level.index
        K, C, D = R[f"K{l}"], R[f"C{l}"], R[f"D{l}"]
        n, rows = level.nz, level.rows
        shape = (rows, LANES)
        lane, row = lanes_of(shape), rows_of(shape)
        zp, zm, yp, ym, xp, xm = bounds(level)
        keep_yp = jnp.where(row == level.ny - 1, yp, 1.0)
        keep_ym = jnp.where(row == 0, ym, 1.0)
        keep_xp = jnp.where(lane == level.nx - 1, xp, 1.0)
        keep_xm = jnp.where(lane == 0, xm, 1.0)

        def step(z, carry):
            ze = z + 1

            def at(comp, dz=0, dy=0):
                return K[comp, ze + dz, pl.ds(RO + dy, rows), :]

            def along(comp, which, sign):
                value = at(comp)
                if level.split:
                    halo = R[f"KH{l}"][which, z]
                    value = jnp.where(lane == (level.right if sign > 0 else LANES - 1), halo, value)
                return roll(value, LANES - 1 if sign > 0 else 1)

            keep_zp = jnp.where(z == n - 1, zp, 1.0)
            keep_zm = jnp.where(z == 0, zm, 1.0)
            keep = ((keep_zp, keep_zm), (keep_yp, keep_ym), (keep_xp, keep_xm))
            weights = (
                (0.5 * (at(0) + at(0, 1)), 0.5 * (at(0) + at(0, -1))),
                (0.5 * (at(1) + at(1, 0, 1)), 0.5 * (at(1) + at(1, 0, -1))),
                (0.5 * (at(2) + along(2, 0, 1)), 0.5 * (at(2) + along(2, 0, -1))),
            )
            total = weights[0][0] + weights[0][1] + weights[1][0] + weights[1][1] + weights[2][0] + weights[2][1]
            diagonal = 1.0 + level.tau * total
            inverse = relax / diagonal
            scale = level.tau * inverse
            D[0, z] = inverse
            D[1, z] = diagonal * (1.0 / relax)
            for a in range(3):
                for s in range(2):
                    C[2 * a + s, z] = scale * weights[a][s] * keep[a][s]
            quarter = 0.25 * scale

            def shifted(comp, axis, sign):
                if axis == 0:
                    return at(comp, sign)
                if axis == 1:
                    return at(comp, 0, sign)
                return along(comp, 1 if comp == 4 else 2, sign)

            for number, (a, b, comp) in enumerate(PAIRS):
                ka = [shifted(comp, a, 1), shifted(comp, a, -1)]
                kb = [shifted(comp, b, 1), shifted(comp, b, -1)]
                for sa in range(2):
                    for sb in range(2):
                        value = quarter * (ka[sa] + kb[sb]) * keep[a][sa] * keep[b][sb]
                        C[6 + 4 * number + 2 * sa + sb, z] = value if sa == sb else -value
            return carry

        lax.fori_loop(0, n, step, 0)

    def sweep(level, source, emit, halo=True):
        l = level.index
        V, C, G, XP, XM = R[f"V{l}"], R[f"C{l}"], R[f"G{l}"], R[f"XP{l}"], R[f"XM{l}"]
        rows = level.rows

        def shift(ze, carry):
            value = V[source, ze]
            up = down = value
            if halo:
                lane = lanes_of(value.shape)
                edge = R[f"H{l}"][source, ze]
                up = jnp.where(lane == level.right, edge, value)
                down = jnp.where(lane == LANES - 1, edge, value)
            XP[ze] = roll(up, LANES - 1)
            XM[ze] = roll(down, 1)
            return carry

        lax.fori_loop(0, level.nz + 2, shift, 0)

        def step(z, carry):
            ze = z + 1

            def at(dz, dy, dx):
                where_rows = pl.ds(RO + dy, rows)
                if dx == 0:
                    return V[source, ze + dz, where_rows, :]
                return (XP if dx > 0 else XM)[ze + dz, where_rows, :]

            center = at(0, 0, 0)
            parts = [G[z] - relax * center, None, None]
            offsets = [(1, 0, 0), (-1, 0, 0), (0, 1, 0), (0, -1, 0), (0, 0, 1), (0, 0, -1)]
            for a, b, _ in PAIRS:
                for sa in (1, -1):
                    for sb in (1, -1):
                        offset = [0, 0, 0]
                        offset[a], offset[b] = sa, sb
                        offsets.append(tuple(offset))
            for number, offset in enumerate(offsets):
                term = C[number, z] * at(*offset)
                slot = number % 3
                parts[slot] = term if parts[slot] is None else parts[slot] + term
            emit(z, center, (parts[0] + parts[1]) + parts[2])
            return carry

        lax.fori_loop(0, level.nz, step, 0)

    def into(level, slot):
        V = R[f"V{level.index}"]

        def emit(z, value, delta):
            V[slot, z + 1, pl.ds(RO, level.rows), :] = value + delta

        return emit

    pending = []
    count = [0]

    def drain():
        for copy in pending:
            copy.wait_send()
        pending.clear()

    def exchange(level, slot, step, during=None):
        l = level.index
        V, H, YB, PB, X = R[f"V{l}"], R[f"H{l}"], R[f"YB{l}"], R[f"PB{l}"], R["PX"]
        ZB = R[f"ZB{l}"]
        RZ, RY, RP = R[f"RZ{l}"], R[f"RY{l}"], R[f"RP{l}"]
        nz, ny, rows, zrows = level.nz, level.ny, level.rows, level.zrows
        drain()
        for z in range(nz):
            YB[0, pl.ds(z, 1), :] = V[slot, z + 1, pl.ds(RO, 1), :]
            YB[1, pl.ds(z, 1), :] = V[slot, z + 1, pl.ds(RO + ny - 1, 1), :]
        ZB[0] = V[slot, 1, pl.ds(RO, rows), :]
        ZB[1] = V[slot, nz, pl.ds(RO, rows), :]
        PB[...] = pack_x(level, lambda z: V[slot, z + 1, pl.ds(RO, rows), :])
        parity = count[0] % 2
        count[0] += 1
        copies = []
        ylow, zlow = rows - 8, zrows - 8
        for number, (kind, where, (ox, oy, oz)) in enumerate(MESSAGES):
            if kind == "z":
                src, dst = ZB.at[0 if where else 1], RZ.at[step, where]
            elif kind == "y":
                face = where // 3
                if where % 3 == 0:
                    src, dst = YB.at[face], RY.at[step, where]
                else:
                    low = 0 if where % 3 == 1 else zlow
                    src, dst = YB.at[face, pl.ds(low, 8)], RY.at[step, where, pl.ds(0, 8)]
            else:
                part = where % 5
                if part in (1, 2):
                    low = 0 if part == 1 else ylow
                    src, dst = PB.at[pl.ds(low, 8)], RP.at[step, where, pl.ds(0, 8)]
                else:
                    src, dst = PB, RP.at[step, where]
            copy = pltpu.make_async_remote_copy(
                src_ref=src, dst_ref=dst, send_sem=R["send"].at[number], recv_sem=R["recv"].at[parity, number],
                device_id=device(ox, oy, oz), device_id_type=MESH,
            )
            copy.start()
            copies.append(copy)
        pending.extend(copies)
        if during is not None:
            during()
        for copy in copies:
            copy.wait_recv()
        V[slot, nz + 1, pl.ds(RO, rows), :] = RZ[step, 1]
        V[slot, 0, pl.ds(RO, rows), :] = RZ[step, 0]
        for face in range(2):
            place = RO + ny if face == 0 else RO - 1
            for z in range(nz):
                V[slot, z + 1, pl.ds(place, 1), :] = RY[step, 3 * face, pl.ds(z, 1), :]
            V[slot, nz + 1, pl.ds(place, 1), :] = RY[step, 3 * face + 1, pl.ds(0, 1), :]
            V[slot, 0, pl.ds(place, 1), :] = RY[step, 3 * face + 2, pl.ds(nz - 1 - zlow, 1), :]

        def merged(part, size):
            even = lanes_of((size, LANES)) % 2 == 0
            return jnp.where(even, RP[step, part, pl.ds(0, size), :], RP[step, 5 + part, pl.ds(0, size), :])

        lane = lanes_of((rows, LANES))
        middle = merged(0, rows)
        above = roll(merged(3, rows), 2 * nz)
        below = roll(merged(4, rows), -2 * nz)

        def slab_lanes(ze):
            return (lane == (level.right + 2 * ze) % LANES) | (lane == (2 * ze + LANES - 1) % LANES)

        middle = jnp.where(slab_lanes(nz + 1), above, jnp.where(slab_lanes(0), below, middle))
        size = level.stride
        X[pl.ds(RO, rows), :] = middle
        X[pl.ds(RO + ny, 1), :] = merged(1, 8)[0:1]
        X[pl.ds(RO - 1, 1), :] = merged(2, 8)[ny - 1 - ylow : ny - ylow]
        whole = X[pl.ds(0, size), :]
        for ze in range(nz + 2):
            H[slot, ze] = roll(whole, -2 * ze)

    def start_faces(level):
        l = level.index
        K, KY, KP, KZ = R[f"K{l}"], R[f"KY{l}"], R[f"KP{l}"], R[f"KZ{l}"]
        nz, ny, rows = level.nz, level.ny, level.rows
        for i, comp in enumerate((0, 3, 4)):
            KZ[0, i] = K[comp, 1, pl.ds(RO, rows), :]
            KZ[1, i] = K[comp, nz, pl.ds(RO, rows), :]
        for i, comp in enumerate((1, 3, 5)):
            for z in range(nz):
                KY[0, i, pl.ds(z, 1), :] = K[comp, z + 1, pl.ds(RO, 1), :]
                KY[1, i, pl.ds(z, 1), :] = K[comp, z + 1, pl.ds(RO + ny - 1, 1), :]
        for i, comp in enumerate((2, 4, 5)):
            KP[i] = pack_x(level, lambda z: K[comp, z + 1, pl.ds(RO, rows), :])
        copies = []
        for number, (kind, where, (ox, oy, oz)) in enumerate(FACES):
            if kind == "z":
                src, dst = KZ.at[0 if where else 1], R[f"RKZ{l}"].at[where]
            elif kind == "y":
                src, dst = KY.at[where], R[f"RKY{l}"].at[where]
            else:
                src, dst = KP, R[f"RKP{l}"].at[where]
            copy = pltpu.make_async_remote_copy(
                src_ref=src, dst_ref=dst, send_sem=R["ksend"].at[l, number], recv_sem=R["krecv"].at[l, number],
                device_id=device(ox, oy, oz), device_id_type=MESH,
            )
            copy.start()
            copies.append(copy)
        return copies

    def finish_faces(level, copies):
        l = level.index
        K, KH = R[f"K{l}"], R[f"KH{l}"]
        nz, ny, rows = level.nz, level.ny, level.rows
        for copy in copies:
            copy.wait()
        for i, comp in enumerate((0, 3, 4)):
            K[comp, nz + 1, pl.ds(RO, rows), :] = R[f"RKZ{l}"][1, i] * in_zp
            K[comp, 0, pl.ds(RO, rows), :] = R[f"RKZ{l}"][0, i] * in_zm
        for i, comp in enumerate((1, 3, 5)):
            for z in range(nz):
                K[comp, z + 1, pl.ds(RO + ny, 1), :] = R[f"RKY{l}"][0, i, pl.ds(z, 1), :] * in_yp
                K[comp, z + 1, pl.ds(RO - 1, 1), :] = R[f"RKY{l}"][1, i, pl.ds(z, 1), :] * in_ym
        even = lanes_of((rows, LANES)) % 2 == 0
        for i in range(3):
            both = jnp.where(even, R[f"RKP{l}"][0, i] * in_xp, R[f"RKP{l}"][1, i] * in_xm)
            for z in range(nz):
                KH[i, z] = roll(both, -2 * (z + 1))

    class Gather:
        def __init__(self, tag, comps):
            self.tag, self.comps = tag, comps
            self.copies = []

        def send(self, phase, src, dst_of, targets):
            self.copies = []
            for number, offset in enumerate(targets):
                copy = pltpu.make_async_remote_copy(
                    src_ref=src, dst_ref=dst_of(number), send_sem=R[f"gs{self.tag}"].at[phase, number],
                    recv_sem=R[f"gr{self.tag}"].at[phase, number], device_id=device(*offset), device_id_type=MESH,
                )
                copy.start()
                self.copies.append(copy)

        def wait(self):
            for copy in self.copies:
                copy.wait()

        def phase_x(self, tiles):
            own, received = R[f"GX{self.tag}"], R[f"RX{self.tag}"]
            own[...] = tiles
            self.send(0, own, lambda number: received.at[number], [(k, 0, 0) for k in range(1, GX)])

        def phase_y(self):
            self.wait()
            slots = R[f"RY{self.tag}"]
            total = R[f"GX{self.tag}"][...]
            for k in range(GX - 1):
                total = total + R[f"RX{self.tag}"][k]
            slots[gy] = total
            self.send(1, slots.at[gy], lambda number: slots.at[gy], [(0, k, 0) for k in range(1, GY)])

        def phase_z(self):
            self.wait()
            slots, out = R[f"RY{self.tag}"], R[f"RZ{self.tag}"]
            for i in range(self.comps):
                for y in range(GY):
                    out[gz, i, pl.ds(2 * y, 2), :] = slots[y, pl.ds(2 * i, 2), :]
            self.send(2, out.at[gz], lambda number: out.at[gz], [(0, 0, k) for k in range(1, GZ)])

        def finish(self, store):
            self.wait()
            out = R[f"RZ{self.tag}"]
            for i in range(self.comps):
                for z in range(GZ):
                    value = out[z, i]
                    left = lanes_of(value.shape) < 64
                    store(i, 2 * z, jnp.where(left, value, 0.0))
                    store(i, 2 * z + 1, jnp.where(left, roll(value, 64), 0.0))

    def own_tile(values, comps, total_rows):
        T = R["tile"]
        T[...] = jnp.zeros(T.shape, F32)
        for i in range(comps):
            low = values[(2 * i) * 8 : (2 * i) * 8 + 8]
            high = values[(2 * i + 1) * 8 : (2 * i + 1) * 8 + 8]
            T[pl.ds(2 * i, 2), :] = (low + roll(high, 64))[0:2]
        return roll(T[pl.ds(0, total_rows), :], 16 * gx)

    L0, L1, L2, L3, L4 = levels
    for level in (L3, L4):
        for name in ("K", "V"):
            ref = R[f"{name}{level.index}"]
            for i in range(ref.shape[0]):
                ref[i] = jnp.zeros(ref.shape[1:], F32)

    def fill(z, carry):
        weight = R["tissue"][z].astype(F32)
        for comp in range(3):
            R["K0"][comp, z + 1, pl.ds(RO, L0.rows), :] = R["conduct"][comp, z] * weight
            R["K0"][3 + comp, z + 1, pl.ds(RO, L0.rows), :] = R["cross"][comp, z] * weight
        return carry

    lax.fori_loop(0, L0.nz, fill, 0)
    pl.semaphore_wait(barrier, len(unique))
    faces0 = start_faces(L0)

    def coarser_tensor(level, lower):
        coarsen_rows(level, lower, lambda i, z, rows: R[f"K{level.index}"][i, z + 1, rows, :], 6)
        height = (level.nz // 2) * lower.rows
        values = coarsen_lanes(level, 6 * height)
        if lower.split:
            for i in range(6):
                for z in range(lower.nz):
                    start = i * height + z * lower.rows
                    R[f"K{lower.index}"][i, z + 1, pl.ds(RO, lower.rows), :] = values[start : start + lower.rows]
        return values

    R["stage"][...] = jnp.zeros(R["stage"].shape, F32)
    coarser_tensor(L0, L1)
    faces1 = start_faces(L1)
    coarser_tensor(L1, L2)
    faces2 = start_faces(L2)
    block3 = Level(3, 2, 2, 16, False)
    gather_k = Gather("k", 6)
    gather_k.phase_x(own_tile(coarser_tensor(L2, block3), 6, 16))

    zl = R["src_z"][...] - gz * L0.nz
    yl = R["src_y"][...] - gy * L0.ny
    xl = R["src_x"][...] - gx * L0.nx
    inside = (zl >= 0) & (zl < L0.nz) & (yl >= 0) & (yl < L0.ny)
    R["key"][0:1, :] = jnp.where(inside, zl * L0.ny + yl, -1)
    R["key"][1:2, :] = xl
    R["counts"][...] = jnp.zeros(R["counts"].shape, F32)
    chunk = 256

    def scatter(i, carry):
        start = pl.multiple_of(i * chunk, chunk)
        key = R["key"][0:1, pl.ds(start, chunk)]
        key_x = R["key"][1:2, pl.ds(start, chunk)]
        left = jnp.where(rows_of((L0.nz * L0.ny, chunk)) == key, 1.0, 0.0).astype(jnp.bfloat16)
        right = jnp.where(rows_of((LANES, chunk)) == key_x, 1.0, 0.0).astype(jnp.bfloat16)
        R["counts"][...] += lax.dot_general(left, right, (((1,), (1,)), ((), ())), preferred_element_type=F32)
        return carry

    lax.fori_loop(0, sources // chunk, scatter, 0)

    finish_faces(L0, faces0)
    coefficients(L0)

    def load0(z):
        return stim_height * R["counts"][pl.ds(pl.multiple_of(z * L0.ny, 8), L0.rows), :]

    def first_sweep(level, load):
        l = level.index

        def step(z, carry):
            value = load(z) * R[f"D{l}"][0, z]
            R[f"G{l}"][z] = value
            R[f"V{l}"][0, z + 1, pl.ds(RO, level.rows), :] = value
            return carry

        lax.fori_loop(0, level.nz, step, 0)

    def residual(level, slot, halo=True):
        l = level.index
        store = R[f"XR{l}"]

        def emit(z, value, delta):
            store[z, pl.ds(RO, level.rows), :] = delta * R[f"D{l}"][1, z]

        sweep(level, slot, emit, halo)

    def restricted(level, lower):
        coarsen_rows(level, lower, lambda i, z, rows: R[f"XR{level.index}"][z, rows, :], 1)
        return coarsen_lanes(level, (level.nz // 2) * lower.rows)

    def during_01():
        gather_k.phase_y()
        finish_faces(L1, faces1)
        coefficients(L1)

    def during_02():
        gather_k.phase_z()
        finish_faces(L2, faces2)
        coefficients(L2)

    def coarse_setup():
        def store(i, z, value):
            R["K3"][i, z + 1, pl.ds(RO, L3.rows), :] = clean(L3, value)

        gather_k.finish(store)
        coefficients(L3)
        coarsen_rows(L3, L4, lambda i, z, rows: R["K3"][i, z + 1, rows, :], 6)
        height = L4.nz * L4.rows
        values = coarsen_lanes(L3, 6 * height)
        for i in range(6):
            for z in range(L4.nz):
                start = i * height + z * L4.rows
                R["K4"][i, z + 1, pl.ds(RO, L4.rows), :] = clean(L4, values[start : start + L4.rows])
        coefficients(L4)

    during = {(0, 0): during_01, (0, 1): during_02, (2, 0): coarse_setup}

    first_sweep(L0, load0)
    for level, lower in ((L0, L1), (L1, L2), (L2, block3)):
        l = level.index
        exchange(level, 0, 0, during.get((l, 0)))
        sweep(level, 0, into(level, 1))
        exchange(level, 1, 1, during.get((l, 1)))
        residual(level, 1)
        values = restricted(level, lower)
        if lower.split:
            R["load"][pl.ds(0, lower.nz * lower.rows), :] = values
            first_sweep(lower, lambda z: R["load"][pl.ds(pl.multiple_of(z * lower.rows, 8), lower.rows), :])

    gather_f = Gather("f", 1)
    gather_f.phase_x(own_tile(values, 1, 8))
    gather_f.phase_y()
    gather_f.phase_z()

    def store_load(i, z, value):
        R["load"][pl.ds(z * L3.rows, L3.rows), :] = value

    gather_f.finish(store_load)

    def load_of(level):
        return lambda z: clean(level, R["load"][pl.ds(pl.multiple_of(z * level.rows, 8), level.rows), :])

    first_sweep(L3, load_of(L3))
    sweep(L3, 0, into(L3, 1), False)
    residual(L3, 1, False)
    values = restricted(L3, L4)
    R["load"][pl.ds(0, L4.nz * L4.rows), :] = values
    first_sweep(L4, load_of(L4))
    for i in range(COARSE - 1):
        sweep(L4, i % 2, into(L4, (i + 1) % 2), False)
    last4 = (COARSE - 1) % 2

    def spread(level, nz_c, ny_c, nx_c, stride_c, get, base, halo):
        l = level.index
        M, PV = R["merge"], R["spread"]
        a, b = rows_of((LANES, LANES)), lanes_of((LANES, LANES))
        main = (a == b // 2) & (b < level.nx)
        edges = ((a == nx_c) & (b == level.right)) | ((a == LANES - 1) & (b == LANES - 1))
        wide = halo and level.nx == LANES
        if halo and not wide:
            main = main | edges
        height = (nz_c + 2) * stride_c
        stacked = jnp.concatenate([get(ze) for ze in range(nz_c + 2)], axis=0)
        M[0, pl.ds(0, height), :] = dot(stacked, jnp.where(main, 1.0, 0.0).astype(F32))
        if wide:
            M[1, pl.ds(0, height), :] = dot(stacked, jnp.where(edges, 1.0, 0.0).astype(F32))
        V = R[f"V{l}"]
        for layer in range(2 if wide else 1):
            for ze in range(nz_c + 2):
                value = M[layer, pl.ds(ze * stride_c + RO - 1, ny_c + 2), :]
                slabs = [zf for zf in (2 * ze - 1, 2 * ze) if 0 <= zf <= level.nz + 1]
                for phase in range(2):
                    PV[layer, ze, pl.ds(RO - 2 + phase, ny_c + 2, stride=2), :] = value
        for ze in range(nz_c + 2):
            for zf in (2 * ze - 1, 2 * ze):
                if 0 <= zf <= level.nz + 1:
                    size = level.stride
                    V[2, zf] = V[1, zf] + PV[0, ze, pl.ds(0, size), :]
                    if halo:
                        H = R[f"H{l}"]
                        H[2, zf] = H[1, zf] + PV[1 if wide else 0, ze, pl.ds(0, size), :]

    def coarse_slab(level, slot):
        V = R[f"V{level.index}"]

        def get(ze):
            value = V[slot, ze]
            if level.split:
                lane = lanes_of(value.shape)
                edge = (lane == level.right) | (lane == LANES - 1)
                value = jnp.where(edge, R[f"H{level.index}"][slot, ze], value)
            return value

        return get

    spread(L3, L4.nz, L4.ny, L4.nx, L4.stride, coarse_slab(L4, last4), 0, False)
    sweep(L3, 2, into(L3, 0), False)
    sweep(L3, 0, into(L3, 1), False)

    def own_slab(ze):
        value = R["V3"][1, 2 * gz + ze]
        value = roll(value, L3.stride - 2 * gy, axis=0)
        value = roll(value, LANES - 16 * gx)
        return value[0:24]

    spread(L2, 2, 2, 16, 24, own_slab, 0, True)
    for level in (L2, L1):
        sweep(level, 2, into(level, 3))
        exchange(level, 3, 2)
        sweep(level, 3, into(level, 0))
        exchange(level, 0, 3)
        finer = levels[level.index - 1]
        spread(finer, level.nz, level.ny, level.nx, level.stride, coarse_slab(level, 0), 0, True)
    sweep(L0, 2, into(L0, 3))
    exchange(L0, 3, 2)

    def emit_out(z, value, delta):
        R["out"][z] = value + delta

    sweep(L0, 3, emit_out)
    drain()


def solution(mesh):
    sizes = (mesh.shape["gx"], mesh.shape["gy"], mesh.shape["gz"])
    GX, GY, GZ = sizes

    def body(conduct, cross, tissue, src_z, src_y, src_x):
        nz, ny, nx = tissue.shape
        sources = src_z.shape[0]
        levels = [Level(l, nz >> l, ny >> l, nx >> l, True) for l in range(3)]
        levels.append(Level(3, 2 * GZ, 2 * GY, 16 * GX, False))
        levels.append(Level(4, GZ, GY, 8 * GX, False))
        scratch = {}

        def vmem(name, *shape, dtype=F32):
            scratch[name] = pltpu.VMEM(shape, dtype)

        for level in levels:
            l, z, rows, stride, zrows = level.index, level.nz, level.rows, level.stride, level.zrows
            slots = 4 if level.split else 3
            vmem(f"K{l}", 6, z + 2, stride, LANES)
            vmem(f"C{l}", 18, z, rows, LANES)
            vmem(f"D{l}", 2, z, rows, LANES)
            vmem(f"G{l}", z, rows, LANES)
            vmem(f"V{l}", slots, z + 2, stride, LANES)
            vmem(f"XP{l}", z + 2, stride, LANES)
            vmem(f"XM{l}", z + 2, stride, LANES)
            vmem(f"XR{l}", z, stride, LANES)
            if level.split:
                vmem(f"H{l}", slots, z + 2, stride, LANES)
                vmem(f"KH{l}", 3, z, rows, LANES)
                vmem(f"YB{l}", 2, zrows, LANES)
                vmem(f"PB{l}", rows, LANES)
                vmem(f"ZB{l}", 2, rows, LANES)
                vmem(f"RZ{l}", 4, 2, rows, LANES)
                vmem(f"RY{l}", 4, 6, zrows, LANES)
                vmem(f"RP{l}", 4, 10, rows, LANES)
                vmem(f"KZ{l}", 2, 3, rows, LANES)
                vmem(f"KY{l}", 2, 3, zrows, LANES)
                vmem(f"KP{l}", 3, rows, LANES)
                vmem(f"RKZ{l}", 2, 3, rows, LANES)
                vmem(f"RKY{l}", 2, 3, zrows, LANES)
                vmem(f"RKP{l}", 2, 3, rows, LANES)
        vmem("PX", levels[0].stride, LANES)
        vmem("stage", 6 * 8 * 8, LANES)
        vmem("tile", 16, LANES)
        vmem("key", 2, sources, dtype=jnp.int32)
        vmem("counts", nz * ny, LANES)
        vmem("load", max(levels[3].nz * levels[3].rows, 64), LANES)
        vmem("merge", 2, 10 * 32, LANES)
        vmem("spread", 2, 10, 48, LANES)
        for tag, comps, height in (("k", 6, 16), ("f", 1, 8)):
            vmem(f"GX{tag}", height, LANES)
            vmem(f"RX{tag}", GX - 1, height, LANES)
            vmem(f"RY{tag}", GY, height, LANES)
            vmem(f"RZ{tag}", GZ, comps, levels[3].rows, LANES)
            most = max(sizes) - 1
            scratch[f"gs{tag}"] = pltpu.SemaphoreType.DMA((3, most))
            scratch[f"gr{tag}"] = pltpu.SemaphoreType.DMA((3, most))
        scratch["send"] = pltpu.SemaphoreType.DMA((len(MESSAGES),))
        scratch["recv"] = pltpu.SemaphoreType.DMA((2, len(MESSAGES)))
        scratch["ksend"] = pltpu.SemaphoreType.DMA((3, len(FACES)))
        scratch["krecv"] = pltpu.SemaphoreType.DMA((3, len(FACES)))
        names = ["conduct", "cross", "tissue", "src_z", "src_y", "src_x", "out"] + list(scratch)
        row = lambda value: value.reshape(1, sources)
        return pl.pallas_call(
            functools.partial(kernel, names, levels, sizes, sources),
            out_shape=jax.ShapeDtypeStruct((nz, ny, nx), F32),
            in_specs=[pl.BlockSpec(memory_space=pltpu.VMEM)] * 6,
            out_specs=pl.BlockSpec(memory_space=pltpu.VMEM),
            scratch_shapes=list(scratch.values()),
            compiler_params=pltpu.CompilerParams(
                collective_id=0, has_side_effects=True, vmem_limit_bytes=60 * 1024 * 1024
            ),
        )(conduct, cross, tissue, row(src_z), row(src_y), row(src_x))

    placed = (P(None, "gz", "gy", "gx"), P(None, "gz", "gy", "gx"), P("gz", "gy", "gx"), P(), P(), P())
    return jax.shard_map(body, mesh=mesh, in_specs=placed, out_specs=P("gz", "gy", "gx"), check_vma=False)
```

profile of v0, /device:TPU:1, one launch (start us, length us, event | category | flops | bytes accessed | tf_op | source)
XLA Modules:
  0.0 117.1 jit_solution(409974841270275917)
XLA Ops:
  0.0 115.5 %shard_map.64 = f32[16,16,128]{2,1,0:T(8,128)} custom-call(f32[3,16,16,128]{3,2,1,0:T(8,128)} %refs_0_.1, f32[3,16,16,128]{3,2,1,0:T(8,128)} %refs_1_.1, s32[16,16,128]{2,1,0:T(8,128)} %refs_2_.1, s32[1,2048]{1,0:T(1,128)} %bitcast.3, s32[1,2048]{1,0:T(1,128)} %bitcast.4, s32[1,2048]{1,0:T(1,128)} %bitcast.5), custom_call_target="tpu_custom_call" | custom-call | tf_op jit(solution)/shard_map/pallas_call | solution.py:720
  115.5 1.6 %copy.8 = f32[16,16,128]{2,1,0:T(8,128)} copy(f32[16,16,128]{2,1,0:T(8,128)} %shard_map.64) | data formatting | bytes 262144
where the time goes:
time: 117 us
  Pallas kernels  116 us (99%)
  local copies, waits for them, and re-layouts  1.57 us (1%)
    pallas_call x1, Pallas kernels, body(): pl.pallas_call(functools.partial(kernel, names, levels, sizes, sources),...  116 us

commit v1 on v0

--- a/solution.py
+++ b/solution.py
@@ -186,7 +186,7 @@
                         C[6 + 4 * number + 2 * sa + sb, z] = value if sa == sb else -value
             return carry
 
-        lax.fori_loop(0, n, step, 0)
+        lax.fori_loop(0, n, step, 0, unroll=min(n, 4))
 
     def sweep(level, source, emit, halo=True):
         l = level.index
@@ -205,7 +205,7 @@
             XM[ze] = roll(down, 1)
             return carry
 
-        lax.fori_loop(0, level.nz + 2, shift, 0)
+        lax.fori_loop(0, level.nz + 2, shift, 0, unroll=level.nz + 2)
 
         def step(z, carry):
             ze = z + 1
@@ -232,7 +232,7 @@
             emit(z, center, (parts[0] + parts[1]) + parts[2])
             return carry
 
-        lax.fori_loop(0, level.nz, step, 0)
+        lax.fori_loop(0, level.nz, step, 0, unroll=min(level.nz, 8))
 
     def into(level, slot):
         V = R[f"V{level.index}"]
@@ -447,7 +447,7 @@
             R["K0"][3 + comp, z + 1, pl.ds(RO, L0.rows), :] = R["cross"][comp, z] * weight
         return carry
 
-    lax.fori_loop(0, L0.nz, fill, 0)
+    lax.fori_loop(0, L0.nz, fill, 0, unroll=4)
     pl.semaphore_wait(barrier, len(unique))
     faces0 = start_faces(L0)
 
@@ -489,7 +489,7 @@
         R["counts"][...] += lax.dot_general(left, right, (((1,), (1,)), ((), ())), preferred_element_type=F32)
         return carry
 
-    lax.fori_loop(0, sources // chunk, scatter, 0)
+    lax.fori_loop(0, sources // chunk, scatter, 0, unroll=2)
 
     finish_faces(L0, faces0)
     coefficients(L0)
@@ -506,7 +506,7 @@
             R[f"V{l}"][0, z + 1, pl.ds(RO, level.rows), :] = value
             return carry
 
-        lax.fori_loop(0, level.nz, step, 0)
+        lax.fori_loop(0, level.nz, step, 0, unroll=min(level.nz, 8))
 
     def residual(level, slot, halo=True):
         l = level.index

time: 117 us -> 90.6 us (0.77)
  Pallas kernels: 116 us -> 89 us
    pallas_call x1, Pallas kernels: 116 us -> 89 us  [body(): pl.pallas_call(functools.partial(kernel, names, levels, sizes, sources),...]
where the time goes in v1:
time: 90.6 us; the launch traced here: 90.5 us
  Pallas kernels  89 us (98%)
  local copies, waits for them, and re-layouts  1.57 us (2%)
    pallas_call x1, Pallas kernels, body(): pl.pallas_call(functools.partial(kernel, names, levels, sizes, sources),...  89 us

profile of v1, /device:TPU:1, one launch (start us, length us, event | category | flops | bytes accessed | tf_op | source)
XLA Modules:
  0.0 90.5 jit_solution(5195638672313017604)
XLA Ops:
  0.0 89.0 %shard_map.64 = f32[16,16,128]{2,1,0:T(8,128)} custom-call(f32[3,16,16,128]{3,2,1,0:T(8,128)} %refs_0_.1, f32[3,16,16,128]{3,2,1,0:T(8,128)} %refs_1_.1, s32[16,16,128]{2,1,0:T(8,128)} %refs_2_.1, s32[1,2048]{1,0:T(1,128)} %bitcast.3, s32[1,2048]{1,0:T(1,128)} %bitcast.4, s32[1,2048]{1,0:T(1,128)} %bitcast.5), custom_call_target="tpu_custom_call" | custom-call | tf_op jit(solution)/shard_map/pallas_call | solution.py:720
  89.0 1.6 %copy.8 = f32[16,16,128]{2,1,0:T(8,128)} copy(f32[16,16,128]{2,1,0:T(8,128)} %shard_map.64) | data formatting | bytes 262144

commit v2 on v1

--- a/solution.py
+++ b/solution.py
@@ -19,8 +19,8 @@
 
 
 class Level:
-    def __init__(self, index, nz, ny, nx, split):
-        self.index, self.nz, self.ny, self.nx, self.split = index, nz, ny, nx, split
+    def __init__(self, index, nz, ny, nx, split, region=False):
+        self.index, self.nz, self.ny, self.nx, self.split, self.region = index, nz, ny, nx, split, region
         self.rows = max(8, -(-ny // 8) * 8)
         self.zrows = max(8, -(-nz // 8) * 8)
         self.stride = RO + self.rows + 8
@@ -58,6 +58,7 @@
 for _side, _ox in ((0, -1), (1, 1)):
     for _part, (_oy, _oz) in enumerate(((0, 0), (-1, 0), (1, 0), (0, -1), (0, 1))):
         MESSAGES.append(("p", 5 * _side + _part, (_ox, _oy, _oz)))
+AROUND = [(dx, dy, dz) for dz in (-1, 0, 1) for dy in (-1, 0, 1) for dx in (-1, 0, 1) if (dx, dy, dz) != (0, 0, 0)]
 FACES = [("z", 1, (0, 0, -1)), ("z", 0, (0, 0, 1)), ("y", 0, (0, -1, 0)), ("y", 1, (0, 1, 0)), ("p", 0, (-1, 0, 0)), ("p", 1, (1, 0, 0))]
 
 
@@ -69,7 +70,7 @@
     def device(ox, oy, oz):
         return (lax.rem(gx + (ox + GX), GX), lax.rem(gy + (oy + GY), GY), lax.rem(gz + (oz + GZ), GZ))
 
-    peers = [offset for _, _, offset in MESSAGES]
+    peers = list(AROUND)
     peers += [(k, 0, 0) for k in range(1, GX)] + [(0, k, 0) for k in range(1, GY)] + [(0, 0, k) for k in range(1, GZ)]
     seen, unique = set(), []
     for ox, oy, oz in peers:
@@ -95,6 +96,15 @@
         if level.split:
             return in_zp, in_zm, in_yp, in_ym, in_xp, in_xm
         return (jnp.zeros((), F32),) * 6
+
+    def inside(level, z):
+        third_z, third_y, third_x = level.nz // 3, level.ny // 3, level.nx // 3
+        shape = (level.rows, LANES)
+        lane, row = lanes_of(shape), rows_of(shape)
+        mask_z = jnp.where(z < third_z, in_zm, jnp.where(z >= 2 * third_z, in_zp, 1.0))
+        mask_y = jnp.where(row < third_y, in_ym, jnp.where(row >= 2 * third_y, in_yp, 1.0))
+        mask_x = jnp.where(lane < third_x, in_xm, jnp.where(lane >= 2 * third_x, in_xp, 1.0))
+        return jnp.where((row < level.ny) & (lane < level.nx), mask_z * mask_y * mask_x, 0.0)
 
     def pack_x(level, get):
         shape = (level.rows, LANES)
@@ -117,13 +127,13 @@
                 total = None
                 for dz in range(2):
                     for dy in range(2):
-                        piece = get(i, 2 * z + dz, pl.ds(RO + dy, half, stride=2))
+                        piece = get(i, 2 * z + dz, dy, half)
                         total = piece if total is None else total + piece
                 stage[pl.ds((i * (level.nz // 2) + z) * lower.rows, half), :] = total
 
-    def coarsen_lanes(level, rows):
+    def coarsen_lanes(level, rows, first=0):
         a, b = rows_of((LANES, LANES)), lanes_of((LANES, LANES))
-        matrix = jnp.where((b == a // 2) & (b < level.nx // 2), 0.125, 0.0).astype(F32)
+        matrix = jnp.where((b == (a - first) // 2) & (a >= first) & (b < level.nx // 2), 0.125, 0.0).astype(F32)
         return dot(R["stage"][pl.ds(0, rows), :], matrix)
 
     def coefficients(level):
@@ -163,6 +173,8 @@
             diagonal = 1.0 + level.tau * total
             inverse = relax / diagonal
             scale = level.tau * inverse
+            if level.region:
+                scale = scale * inside(level, z)
             D[0, z] = inverse
             D[1, z] = diagonal * (1.0 / relax)
             for a in range(3):
@@ -188,7 +200,7 @@
 
         lax.fori_loop(0, n, step, 0, unroll=min(n, 4))
 
-    def sweep(level, source, emit, halo=True):
+    def sweep(level, source, emit, halo=True, first=0, last=None):
         l = level.index
         V, C, G, XP, XM = R[f"V{l}"], R[f"C{l}"], R[f"G{l}"], R[f"XP{l}"], R[f"XM{l}"]
         rows = level.rows
@@ -205,7 +217,8 @@
             XM[ze] = roll(down, 1)
             return carry
 
-        lax.fori_loop(0, level.nz + 2, shift, 0, unroll=level.nz + 2)
+        last = level.nz if last is None else last
+        lax.fori_loop(first, last + 2, shift, 0, unroll=last + 2 - first)
 
         def step(z, carry):
             ze = z + 1
@@ -232,7 +245,7 @@
             emit(z, center, (parts[0] + parts[1]) + parts[2])
             return carry
 
-        lax.fori_loop(0, level.nz, step, 0, unroll=min(level.nz, 8))
+        lax.fori_loop(first, last, step, 0, unroll=min(last - first, 8))
 
     def into(level, slot):
         V = R[f"V{level.index}"]
@@ -373,6 +386,43 @@
             for z in range(nz):
                 KH[i, z] = roll(both, -2 * (z + 1))
 
+    def start_around(tag):
+        tag_index = "kfp".index(tag)
+        copies = []
+        for number, (dx, dy, dz) in enumerate(AROUND):
+            copy = pltpu.make_async_remote_copy(
+                src_ref=R[f"TA{tag}"], dst_ref=R[f"RA{tag}"].at[number], send_sem=R["asend"].at[tag_index, number],
+                recv_sem=R["arecv"].at[tag_index, number], device_id=device(-dx, -dy, -dz), device_id_type=MESH,
+            )
+            copy.start()
+            copies.append(copy)
+        return copies
+
+    def finish_around(tag, copies, comps, store):
+        for copy in copies:
+            copy.wait()
+        tile = R[f"TA{tag}"]
+        lane = lanes_of(tile.shape)
+        for dz in (-1, 0, 1):
+            for dy in (-1, 0, 1):
+                row_tiles = []
+                for dx in (-1, 0, 1):
+                    if (dx, dy, dz) == (0, 0, 0):
+                        row_tiles.append(tile[...])
+                        continue
+                    value = R[f"RA{tag}"][AROUND.index((dx, dy, dz))]
+                    valid = None
+                    for d, plus, minus in ((dx, in_xp, in_xm), (dy, in_yp, in_ym), (dz, in_zp, in_zm)):
+                        if d:
+                            factor = plus if d > 0 else minus
+                            valid = factor if valid is None else valid * factor
+                    row_tiles.append(value * valid)
+                for z in range(4):
+                    low, mid, high = (roll(row_tiles[i], 32 * i - 32 * z) for i in range(3))
+                    value = jnp.where(lane < 32, low, jnp.where(lane < 64, mid, jnp.where(lane < 96, high, 0.0)))
+                    for comp in range(comps):
+                        store(comp, 4 * (dz + 1) + z, 4 * (dy + 1), value[4 * comp : 4 * comp + 4])
+
     class Gather:
         def __init__(self, tag, comps):
             self.tag, self.comps = tag, comps
@@ -434,11 +484,7 @@
         return roll(T[pl.ds(0, total_rows), :], 16 * gx)
 
     L0, L1, L2, L3, L4 = levels
-    for level in (L3, L4):
-        for name in ("K", "V"):
-            ref = R[f"{name}{level.index}"]
-            for i in range(ref.shape[0]):
-                ref[i] = jnp.zeros(ref.shape[1:], F32)
+    block2, block3 = Level(2, 4, 4, 32, True), Level(3, 2, 2, 16, False)
 
     def fill(z, carry):
         weight = R["tissue"][z].astype(F32)
@@ -451,31 +497,54 @@
     pl.semaphore_wait(barrier, len(unique))
     faces0 = start_faces(L0)
 
-    def coarser_tensor(level, lower):
-        coarsen_rows(level, lower, lambda i, z, rows: R[f"K{level.index}"][i, z + 1, rows, :], 6)
-        height = (level.nz // 2) * lower.rows
-        values = coarsen_lanes(level, 6 * height)
-        if lower.split:
-            for i in range(6):
-                for z in range(lower.nz):
-                    start = i * height + z * lower.rows
-                    R[f"K{lower.index}"][i, z + 1, pl.ds(RO, lower.rows), :] = values[start : start + lower.rows]
-        return values
-
     R["stage"][...] = jnp.zeros(R["stage"].shape, F32)
-    coarser_tensor(L0, L1)
+
+    def tensor_rows(l, offset):
+        return lambda i, z, dy, n: R[f"K{l}"][i, z + 1, pl.ds(offset + dy, n, stride=2), :]
+
+    coarsen_rows(L0, L1, tensor_rows(0, RO), 6)
+    values = coarsen_lanes(L0, 6 * L1.nz * L1.rows)
+    for i in range(6):
+        for z in range(L1.nz):
+            start = (i * L1.nz + z) * L1.rows
+            R["K1"][i, z + 1, pl.ds(RO, L1.rows), :] = values[start : start + L1.rows]
     faces1 = start_faces(L1)
-    coarser_tensor(L1, L2)
-    faces2 = start_faces(L2)
-    block3 = Level(3, 2, 2, 16, False)
+    coarsen_rows(L1, block2, tensor_rows(1, RO), 6)
+    values = coarsen_lanes(L1, 6 * block2.nz * block2.rows)
+
+    def block2_tile(ref, comps, values):
+        for i in range(comps):
+            total = None
+            for z in range(4):
+                start = (i * 4 + z) * 8
+                piece = roll(values[start : start + 8], 32 * z)
+                total = piece if total is None else total + piece
+            ref[pl.ds(4 * i, 4), :] = total[0:4]
+
+    R["TAf"][...] = jnp.zeros(R["TAf"].shape, F32)
+    R["TAp"][...] = jnp.zeros(R["TAp"].shape, F32)
+    block2_tile(R["TAk"], 6, values)
+    around_k = start_around("k")
+    for i in range(6):
+        for z in range(4):
+            start = (i * 4 + z) * 8
+            R["KB2"][i, z] = values[start : start + 8]
+    coarsen_rows(block2, block3, lambda i, z, dy, n: R["KB2"][i, z, pl.ds(dy, n, stride=2), :], 6)
     gather_k = Gather("k", 6)
-    gather_k.phase_x(own_tile(coarser_tensor(L2, block3), 6, 16))
+    gather_k.phase_x(own_tile(coarsen_lanes(block2, 6 * 2 * 8), 6, 16))
+
+    for level in (L2, L3, L4):
+        for name in ("K", "V"):
+            ref = R[f"{name}{level.index}"]
+            for i in range(ref.shape[0]):
+                ref[i] = jnp.zeros(ref.shape[1:], F32)
+    R["load"][...] = jnp.zeros(R["load"].shape, F32)
 
     zl = R["src_z"][...] - gz * L0.nz
     yl = R["src_y"][...] - gy * L0.ny
     xl = R["src_x"][...] - gx * L0.nx
-    inside = (zl >= 0) & (zl < L0.nz) & (yl >= 0) & (yl < L0.ny)
-    R["key"][0:1, :] = jnp.where(inside, zl * L0.ny + yl, -1)
+    here = (zl >= 0) & (zl < L0.nz) & (yl >= 0) & (yl < L0.ny)
+    R["key"][0:1, :] = jnp.where(here, zl * L0.ny + yl, -1)
     R["key"][1:2, :] = xl
     R["counts"][...] = jnp.zeros(R["counts"].shape, F32)
     chunk = 256
@@ -508,18 +577,21 @@
 
         lax.fori_loop(0, level.nz, step, 0, unroll=min(level.nz, 8))
 
-    def residual(level, slot, halo=True):
+    def residual(level, slot, halo=True, first=0, last=None):
         l = level.index
         store = R[f"XR{l}"]
 
         def emit(z, value, delta):
             store[z, pl.ds(RO, level.rows), :] = delta * R[f"D{l}"][1, z]
 
-        sweep(level, slot, emit, halo)
-
-    def restricted(level, lower):
-        coarsen_rows(level, lower, lambda i, z, rows: R[f"XR{level.index}"][z, rows, :], 1)
-        return coarsen_lanes(level, (level.nz // 2) * lower.rows)
+        sweep(level, slot, emit, halo, first, last)
+
+    def restricted(level, lower, z0=0, y0=0, x0=0):
+        def get(i, z, dy, n):
+            return R[f"XR{level.index}"][z + z0, pl.ds(RO + y0 + dy, n, stride=2), :]
+
+        coarsen_rows(level, lower, get, 1)
+        return coarsen_lanes(level, (level.nz // 2) * lower.rows, x0)
 
     def during_01():
         gather_k.phase_y()
@@ -528,7 +600,12 @@
 
     def during_02():
         gather_k.phase_z()
-        finish_faces(L2, faces2)
+
+    def during_10():
+        def store(i, z, row, value):
+            R["K2"][i, z + 1, pl.ds(RO + row, 4), :] = value
+
+        finish_around("k", around_k, 6, store)
         coefficients(L2)
 
     def coarse_setup():
@@ -537,7 +614,7 @@
 
         gather_k.finish(store)
         coefficients(L3)
-        coarsen_rows(L3, L4, lambda i, z, rows: R["K3"][i, z + 1, rows, :], 6)
+        coarsen_rows(L3, L4, tensor_rows(3, RO), 6)
         height = L4.nz * L4.rows
         values = coarsen_lanes(L3, 6 * height)
         for i in range(6):
@@ -546,22 +623,40 @@
                 R["K4"][i, z + 1, pl.ds(RO, L4.rows), :] = clean(L4, values[start : start + L4.rows])
         coefficients(L4)
 
-    during = {(0, 0): during_01, (0, 1): during_02, (2, 0): coarse_setup}
+    during = {(0, 0): during_01, (0, 1): during_02, (1, 0): during_10, (1, 1): coarse_setup}
 
     first_sweep(L0, load0)
-    for level, lower in ((L0, L1), (L1, L2), (L2, block3)):
+    for level, lower in ((L0, L1), (L1, block2)):
         l = level.index
         exchange(level, 0, 0, during.get((l, 0)))
         sweep(level, 0, into(level, 1))
         exchange(level, 1, 1, during.get((l, 1)))
         residual(level, 1)
         values = restricted(level, lower)
-        if lower.split:
+        if l == 0:
             R["load"][pl.ds(0, lower.nz * lower.rows), :] = values
             first_sweep(lower, lambda z: R["load"][pl.ds(pl.multiple_of(z * lower.rows, 8), lower.rows), :])
 
+    def store_region(i, z, row, value):
+        R["load"][pl.ds(z * L2.rows + row, 4), :] = value
+
+    block2_tile(R["TAf"], 1, values)
+    R["load"][...] = jnp.zeros(R["load"].shape, F32)
+    finish_around("f", start_around("f"), 1, store_region)
+    first_sweep(L2, lambda z: R["load"][pl.ds(pl.multiple_of(z * L2.rows, 8), L2.rows), :])
+    sweep(L2, 0, into(L2, 1), False, 3, 9)
+    residual(L2, 1, False, 4, 8)
+    values = restricted(block2, block3, 4, 4, 32)
+
     gather_f = Gather("f", 1)
     gather_f.phase_x(own_tile(values, 1, 8))
+    tile_lane = lanes_of((8, LANES))
+    total = jnp.zeros((8, LANES), F32)
+    for z in range(4):
+        piece = roll(R["V2"][1, 5 + z, pl.ds(RO + 4, 8), :], 32 * z - 32)
+        total = jnp.where((tile_lane >= 32 * z) & (tile_lane < 32 * z + 32), piece, total)
+    R["TAp"][0:4, :] = total[0:4]
+    around_p = start_around("p")
     gather_f.phase_y()
     gather_f.phase_z()
 
@@ -630,20 +725,38 @@
     sweep(L3, 2, into(L3, 0), False)
     sweep(L3, 0, into(L3, 1), False)
 
-    def own_slab(ze):
-        value = R["V3"][1, 2 * gz + ze]
-        value = roll(value, L3.stride - 2 * gy, axis=0)
-        value = roll(value, LANES - 16 * gx)
-        return value[0:24]
-
-    spread(L2, 2, 2, 16, 24, own_slab, 0, True)
-    for level in (L2, L1):
-        sweep(level, 2, into(level, 3))
-        exchange(level, 3, 2)
-        sweep(level, 3, into(level, 0))
-        exchange(level, 0, 3)
-        finer = levels[level.index - 1]
-        spread(finer, level.nz, level.ny, level.nx, level.stride, coarse_slab(level, 0), 0, True)
+    def store_pre(i, z, row, value):
+        R["V2"][2, z + 1, pl.ds(RO + row, 4), :] = value
+
+    finish_around("p", around_p, 1, store_pre)
+    slabs = []
+    count3 = L3.nz + 2
+    for i in range(6):
+        value = R["V3"][1, lax.rem(2 * gz + (count3 - 1 + i), count3)]
+        value = roll(value, lax.rem(2 * L3.stride - RO + 2 - 2 * gy, L3.stride), axis=0)
+        value = roll(value, lax.rem(LANES + 16 - 16 * gx, LANES))
+        slabs.append(value[0:8])
+    a, b = rows_of((LANES, LANES)), lanes_of((LANES, LANES))
+    copied = dot(jnp.concatenate(slabs, axis=0), jnp.where((a == b // 2) & (b < L2.nx), 1.0, 0.0).astype(F32))
+    for i in range(6):
+        for phase in range(2):
+            R["spread"][0, i, pl.ds(phase, 8, stride=2), :] = copied[8 * i : 8 * i + 8]
+    for z in range(L2.nz):
+        where_rows = pl.ds(RO, L2.rows)
+        added = jnp.where(inside(L2, z) > 0.5, R["spread"][0, z // 2, pl.ds(0, L2.rows), :], 0.0)
+        R["V2"][2, z + 1, where_rows, :] = R["V2"][2, z + 1, where_rows, :] + added
+    sweep(L2, 2, into(L2, 3), False, 2, 10)
+    sweep(L2, 3, into(L2, 0), False, 3, 9)
+
+    def region_slab(ze):
+        return roll(R["V2"][0, 4 + ze, pl.ds(4, 24), :], -32)
+
+    spread(L1, 4, 4, 32, 24, region_slab, 0, True)
+    sweep(L1, 2, into(L1, 3))
+    exchange(L1, 3, 2)
+    sweep(L1, 3, into(L1, 0))
+    exchange(L1, 0, 3)
+    spread(L0, L1.nz, L1.ny, L1.nx, L1.stride, coarse_slab(L1, 0), 0, True)
     sweep(L0, 2, into(L0, 3))
     exchange(L0, 3, 2)
 
@@ -661,7 +774,8 @@
     def body(conduct, cross, tissue, src_z, src_y, src_x):
         nz, ny, nx = tissue.shape
         sources = src_z.shape[0]
-        levels = [Level(l, nz >> l, ny >> l, nx >> l, True) for l in range(3)]
+        levels = [Level(l, nz >> l, ny >> l, nx >> l, True) for l in range(2)]
+        levels.append(Level(2, 12, 12, 96, False, True))
         levels.append(Level(3, 2 * GZ, 2 * GY, 16 * GX, False))
         levels.append(Level(4, GZ, GY, 8 * GX, False))
         scratch = {}
@@ -671,7 +785,7 @@
 
         for level in levels:
             l, z, rows, stride, zrows = level.index, level.nz, level.rows, level.stride, level.zrows
-            slots = 4 if level.split else 3
+            slots = 4 if l < 3 else 3
             vmem(f"K{l}", 6, z + 2, stride, LANES)
             vmem(f"C{l}", 18, z, rows, LANES)
             vmem(f"D{l}", 2, z, rows, LANES)
@@ -695,6 +809,12 @@
                 vmem(f"RKZ{l}", 2, 3, rows, LANES)
                 vmem(f"RKY{l}", 2, 3, zrows, LANES)
                 vmem(f"RKP{l}", 2, 3, rows, LANES)
+        for tag, height in (("k", 24), ("f", 8), ("p", 8)):
+            vmem(f"TA{tag}", height, LANES)
+            vmem(f"RA{tag}", len(AROUND), height, LANES)
+        scratch["asend"] = pltpu.SemaphoreType.DMA((3, len(AROUND)))
+        scratch["arecv"] = pltpu.SemaphoreType.DMA((3, len(AROUND)))
+        vmem("KB2", 6, 4, 8, LANES)
         vmem("PX", levels[0].stride, LANES)
         vmem("stage", 6 * 8 * 8, LANES)
         vmem("tile", 16, LANES)
@@ -713,8 +833,8 @@
             scratch[f"gr{tag}"] = pltpu.SemaphoreType.DMA((3, most))
         scratch["send"] = pltpu.SemaphoreType.DMA((len(MESSAGES),))
         scratch["recv"] = pltpu.SemaphoreType.DMA((2, len(MESSAGES)))
-        scratch["ksend"] = pltpu.SemaphoreType.DMA((3, len(FACES)))
-        scratch["krecv"] = pltpu.SemaphoreType.DMA((3, len(FACES)))
+        scratch["ksend"] = pltpu.SemaphoreType.DMA((2, len(FACES)))
+        scratch["krecv"] = pltpu.SemaphoreType.DMA((2, len(FACES)))
         names = ["conduct", "cross", "tissue", "src_z", "src_y", "src_x", "out"] + list(scratch)
         row = lambda value: value.reshape(1, sources)
         return pl.pallas_call(

time: 90.6 us -> 78.7 us (0.87)
  Pallas kernels: 89 us -> 77 us
    pallas_call x1, Pallas kernels: 89 us -> 77 us  [body(): pl.pallas_call(functools.partial(kernel, names, levels, sizes, sources),...]
where the time goes in v2:
time: 78.7 us; the launch traced here: 78.6 us
  Pallas kernels  77 us (98%)
  local copies, waits for them, and re-layouts  1.57 us (2%)
    pallas_call x1, Pallas kernels, body(): pl.pallas_call(functools.partial(kernel, names, levels, sizes, sources),...  77 us

profile of v2, /device:TPU:1, one launch (start us, length us, event | category | flops | bytes accessed | tf_op | source)
XLA Modules:
  0.0 78.6 jit_solution(4474017918797246482)
XLA Ops:
  0.0 77.0 %shard_map.64 = f32[16,16,128]{2,1,0:T(8,128)} custom-call(f32[3,16,16,128]{3,2,1,0:T(8,128)} %refs_0_.1, f32[3,16,16,128]{3,2,1,0:T(8,128)} %refs_1_.1, s32[16,16,128]{2,1,0:T(8,128)} %refs_2_.1, s32[1,2048]{1,0:T(1,128)} %bitcast.3, s32[1,2048]{1,0:T(1,128)} %bitcast.4, s32[1,2048]{1,0:T(1,128)} %bitcast.5), custom_call_target="tpu_custom_call" | custom-call | tf_op jit(solution)/shard_map/pallas_call | solution.py:840
  77.0 1.6 %copy.8 = f32[16,16,128]{2,1,0:T(8,128)} copy(f32[16,16,128]{2,1,0:T(8,128)} %shard_map.64) | data formatting | bytes 262144

commit v3 on v2

--- a/solution.py
+++ b/solution.py
@@ -19,8 +19,8 @@
 
 
 class Level:
-    def __init__(self, index, nz, ny, nx, split, region=False):
-        self.index, self.nz, self.ny, self.nx, self.split, self.region = index, nz, ny, nx, split, region
+    def __init__(self, index, nz, ny, nx, split, margin=None):
+        self.index, self.nz, self.ny, self.nx, self.split, self.margin = index, nz, ny, nx, split, margin
         self.rows = max(8, -(-ny // 8) * 8)
         self.zrows = max(8, -(-nz // 8) * 8)
         self.stride = RO + self.rows + 8
@@ -98,13 +98,24 @@
         return (jnp.zeros((), F32),) * 6
 
     def inside(level, z):
-        third_z, third_y, third_x = level.nz // 3, level.ny // 3, level.nx // 3
+        mz, my, mx = level.margin
         shape = (level.rows, LANES)
         lane, row = lanes_of(shape), rows_of(shape)
-        mask_z = jnp.where(z < third_z, in_zm, jnp.where(z >= 2 * third_z, in_zp, 1.0))
-        mask_y = jnp.where(row < third_y, in_ym, jnp.where(row >= 2 * third_y, in_yp, 1.0))
-        mask_x = jnp.where(lane < third_x, in_xm, jnp.where(lane >= 2 * third_x, in_xp, 1.0))
+        mask_z = jnp.where(z < mz, in_zm, jnp.where(z >= level.nz - mz, in_zp, 1.0))
+        mask_y = jnp.where(row < my, in_ym, jnp.where(row >= level.ny - my, in_yp, 1.0))
+        mask_x = jnp.where(lane < mx, in_xm, jnp.where(lane >= level.nx - mx, in_xp, 1.0))
         return jnp.where((row < level.ny) & (lane < level.nx), mask_z * mask_y * mask_x, 0.0)
+
+    def valid(dx, dy, dz):
+        factor = None
+        for d, plus, minus in ((dx, in_xp, in_xm), (dy, in_yp, in_ym), (dz, in_zp, in_zm)):
+            if d:
+                one = plus if d > 0 else minus
+                factor = one if factor is None else factor * one
+        return factor
+
+    def times(value, factor):
+        return value if factor is None else value * factor
 
     def pack_x(level, get):
         shape = (level.rows, LANES)
@@ -173,7 +184,7 @@
             diagonal = 1.0 + level.tau * total
             inverse = relax / diagonal
             scale = level.tau * inverse
-            if level.region:
+            if level.margin:
                 scale = scale * inside(level, z)
             D[0, z] = inverse
             D[1, z] = diagonal * (1.0 / relax)
@@ -411,17 +422,94 @@
                         row_tiles.append(tile[...])
                         continue
                     value = R[f"RA{tag}"][AROUND.index((dx, dy, dz))]
-                    valid = None
-                    for d, plus, minus in ((dx, in_xp, in_xm), (dy, in_yp, in_ym), (dz, in_zp, in_zm)):
-                        if d:
-                            factor = plus if d > 0 else minus
-                            valid = factor if valid is None else valid * factor
-                    row_tiles.append(value * valid)
+                    row_tiles.append(times(value, valid(dx, dy, dz)))
                 for z in range(4):
                     low, mid, high = (roll(row_tiles[i], 32 * i - 32 * z) for i in range(3))
                     value = jnp.where(lane < 32, low, jnp.where(lane < 64, mid, jnp.where(lane < 96, high, 0.0)))
                     for comp in range(comps):
                         store(comp, 4 * (dz + 1) + z, 4 * (dy + 1), value[4 * comp : 4 * comp + 4])
+
+    def start_wide(tag, comps, get):
+        tag_index = "kfp".index(tag)
+        A, B, S, S2 = (R[f"{name}{tag}"] for name in ("WA", "WB", "WS", "WT"))
+        shape = (8, LANES)
+        lane = lanes_of(shape)
+        for c in range(comps):
+            slabs = [get(c, z) for z in range(8)]
+            strip = jnp.zeros(shape, F32)
+            for z in range(8):
+                low, high = 68 + 8 * z, 8 * z
+                strip = jnp.where((lane >= low) & (lane < low + 4), roll(slabs[z], low), strip)
+                strip = jnp.where((lane >= high) & (lane < high + 4), roll(slabs[z], high - 60), strip)
+            S[c] = strip
+            for h in range(2):
+                S2[h, c // 2, pl.ds(4 * (c % 2), 4), :] = strip[4 * h : 4 * h + 4]
+            for p in range(4):
+                pair = slabs[2 * p] + roll(slabs[2 * p + 1], 64)
+                A[p, c] = pair
+                for h in range(2):
+                    B[h, p // 2, c, pl.ds(4 * (p % 2), 4), :] = pair[4 * h : 4 * h + 4]
+        copies = []
+        for number, (dx, dy, dz) in enumerate(AROUND):
+            t, h = int(dz < 0), int(dy < 0)
+            iz, iy, ix = int(dz > 0), int(dy > 0), int(dx > 0)
+            if dx == 0 and dy == 0:
+                src, dst = A.at[pl.ds(2 * t, 2)], R[f"WRA{tag}"].at[iz]
+            elif dx == 0 and dz == 0:
+                src, dst = B.at[h], R[f"WRB{tag}"].at[iy]
+            elif dx == 0:
+                src, dst = B.at[h, t], R[f"WRC{tag}"].at[2 * iy + iz]
+            elif dy == 0:
+                src, dst = S, R[f"WRS{tag}"].at[3 * ix + dz + 1]
+            else:
+                src, dst = S2.at[h], R[f"WRT{tag}"].at[3 * (2 * ix + iy) + dz + 1]
+            copy = pltpu.make_async_remote_copy(
+                src_ref=src, dst_ref=dst, send_sem=R["wsend"].at[tag_index, number],
+                recv_sem=R["wrecv"].at[tag_index, number], device_id=device(-dx, -dy, -dz), device_id_type=MESH,
+            )
+            copy.start()
+            copies.append(copy)
+        return copies
+
+    def finish_wide(tag, copies, comps, load, store):
+        for copy in copies:
+            copy.wait()
+        A = R[f"WA{tag}"]
+        MS = R["strips"]
+        lane8, lane16 = lanes_of((8, LANES)), lanes_of((16, LANES))
+        edge = (lane16 < 4) | ((lane16 >= 68) & (lane16 < 72))
+        for c in range(comps):
+            for dz in (-1, 0, 1):
+                iz = int(dz > 0)
+                zs = range(4, 8) if dz < 0 else range(0, 8) if dz == 0 else range(0, 4)
+                base = {-1: -4, 0: 4, 1: 12}[dz]
+                for z in zs:
+                    tile = A[z // 2, c] if dz == 0 else R[f"WRA{tag}"][iz, z // 2 - (2 if dz < 0 else 0), c]
+                    store(c, z + base, 4, roll(times(tile, valid(0, 0, dz)), 4 - 64 * (z % 2)))
+                for dy in (-1, 1):
+                    iy = int(dy > 0)
+                    for z in zs:
+                        tile = R[f"WRB{tag}"][iy, z // 4, c] if dz == 0 else R[f"WRC{tag}"][2 * iy + iz, c]
+                        part = 4 * ((z % 4) // 2)
+                        piece = roll(times(tile, valid(0, dy, dz)), 4 - 64 * (z % 2))
+                        store(c, z + base, 0 if dy < 0 else 12, piece[part : part + 4])
+                for dy in (-1, 0, 1):
+                    iy = int(dy > 0)
+                    sides = []
+                    for ix, dx in enumerate((-1, 1)):
+                        if dy == 0:
+                            tile = R[f"WRS{tag}"][3 * ix + dz + 1, c]
+                        else:
+                            tile = R[f"WRT{tag}"][3 * (2 * ix + iy) + dz + 1, c // 2]
+                        sides.append(times(tile, valid(dx, dy, dz)))
+                    both = jnp.where(lane8 < 64, sides[0], sides[1])
+                    if dy == 0:
+                        MS[dz + 1, pl.ds(4, 8), :] = both
+                    else:
+                        MS[dz + 1, pl.ds(0 if dy < 0 else 12, 4), :] = both[4 * (c % 2) : 4 * (c % 2) + 4]
+                strip = MS[dz + 1]
+                for z in zs:
+                    store(c, z + base, 0, jnp.where(edge, roll(strip, -8 * z), load(c, z + base)))
 
     class Gather:
         def __init__(self, tag, comps):
@@ -484,7 +572,7 @@
         return roll(T[pl.ds(0, total_rows), :], 16 * gx)
 
     L0, L1, L2, L3, L4 = levels
-    block2, block3 = Level(2, 4, 4, 32, True), Level(3, 2, 2, 16, False)
+    block1, block2, block3 = Level(1, 8, 8, 64, True), Level(2, 4, 4, 32, True), Level(3, 2, 2, 16, False)
 
     def fill(z, carry):
         weight = R["tissue"][z].astype(F32)
@@ -502,15 +590,18 @@
     def tensor_rows(l, offset):
         return lambda i, z, dy, n: R[f"K{l}"][i, z + 1, pl.ds(offset + dy, n, stride=2), :]
 
-    coarsen_rows(L0, L1, tensor_rows(0, RO), 6)
-    values = coarsen_lanes(L0, 6 * L1.nz * L1.rows)
+    coarsen_rows(L0, block1, tensor_rows(0, RO), 6)
+    values = coarsen_lanes(L0, 6 * 8 * 8)
+
+    def slab_of(values):
+        return lambda c, z: values[(c * 8 + z) * 8 : (c * 8 + z) * 8 + 8]
+
+    wide_k = start_wide("k", 6, slab_of(values))
     for i in range(6):
-        for z in range(L1.nz):
-            start = (i * L1.nz + z) * L1.rows
-            R["K1"][i, z + 1, pl.ds(RO, L1.rows), :] = values[start : start + L1.rows]
-    faces1 = start_faces(L1)
-    coarsen_rows(L1, block2, tensor_rows(1, RO), 6)
-    values = coarsen_lanes(L1, 6 * block2.nz * block2.rows)
+        for z in range(8):
+            R["KB1"][i, z] = values[(i * 8 + z) * 8 : (i * 8 + z) * 8 + 8]
+    coarsen_rows(block1, block2, lambda i, z, dy, n: R["KB1"][i, z, pl.ds(dy, n, stride=2), :], 6)
+    values = coarsen_lanes(block1, 6 * 4 * 8)
 
     def block2_tile(ref, comps, values):
         for i in range(comps):
@@ -533,7 +624,7 @@
     gather_k = Gather("k", 6)
     gather_k.phase_x(own_tile(coarsen_lanes(block2, 6 * 2 * 8), 6, 16))
 
-    for level in (L2, L3, L4):
+    for level in (L1, L2, L3, L4):
         for name in ("K", "V"):
             ref = R[f"{name}{level.index}"]
             for i in range(ref.shape[0]):
@@ -593,19 +684,34 @@
         coarsen_rows(level, lower, get, 1)
         return coarsen_lanes(level, (level.nz // 2) * lower.rows, x0)
 
+    def tensor_region(l):
+        def store(i, z, row, value):
+            R[f"K{l}"][i, z + 1, pl.ds(RO + row, value.shape[0]), :] = value
+
+        return store
+
+    def iterate_region(l):
+        def store(i, z, row, value):
+            R[f"V{l}"][2, z + 1, pl.ds(RO + row, value.shape[0]), :] = value
+
+        return store
+
+    def load_region(level):
+        def store(i, z, row, value):
+            R["load"][pl.ds(z * level.rows + row, value.shape[0]), :] = value
+
+        return store
+
     def during_01():
         gather_k.phase_y()
-        finish_faces(L1, faces1)
-        coefficients(L1)
 
     def during_02():
         gather_k.phase_z()
+        finish_wide("k", wide_k, 6, lambda i, z: R["K1"][i, z + 1, pl.ds(RO, 16), :], tensor_region(1))
+        coefficients(L1)
 
     def during_10():
-        def store(i, z, row, value):
-            R["K2"][i, z + 1, pl.ds(RO + row, 4), :] = value
-
-        finish_around("k", around_k, 6, store)
+        finish_around("k", around_k, 6, tensor_region(2))
         coefficients(L2)
 
     def coarse_setup():
@@ -623,27 +729,36 @@
                 R["K4"][i, z + 1, pl.ds(RO, L4.rows), :] = clean(L4, values[start : start + L4.rows])
         coefficients(L4)
 
-    during = {(0, 0): during_01, (0, 1): during_02, (1, 0): during_10, (1, 1): coarse_setup}
+    def load_of(level):
+        return lambda z: clean(level, R["load"][pl.ds(pl.multiple_of(z * level.rows, 8), level.rows), :])
 
     first_sweep(L0, load0)
-    for level, lower in ((L0, L1), (L1, block2)):
-        l = level.index
-        exchange(level, 0, 0, during.get((l, 0)))
-        sweep(level, 0, into(level, 1))
-        exchange(level, 1, 1, during.get((l, 1)))
-        residual(level, 1)
-        values = restricted(level, lower)
-        if l == 0:
-            R["load"][pl.ds(0, lower.nz * lower.rows), :] = values
-            first_sweep(lower, lambda z: R["load"][pl.ds(pl.multiple_of(z * lower.rows, 8), lower.rows), :])
-
-    def store_region(i, z, row, value):
-        R["load"][pl.ds(z * L2.rows + row, 4), :] = value
+    exchange(L0, 0, 0, during_01)
+    sweep(L0, 0, into(L0, 1))
+    exchange(L0, 1, 1, during_02)
+    residual(L0, 1)
+    values = restricted(L0, block1)
+
+    wide_f = start_wide("f", 1, slab_of(values))
+    during_10()
+    finish_wide("f", wide_f, 1, lambda i, z: R["load"][pl.ds(16 * z, 16), :], load_region(L1))
+    first_sweep(L1, load_of(L1))
+    sweep(L1, 0, into(L1, 1), False, 3, 13)
+    residual(L1, 1, False, 4, 12)
+    values = restricted(block1, block2, 4, 4, 4)
 
     block2_tile(R["TAf"], 1, values)
+    around_f = start_around("f")
+    lane8 = lanes_of((8, LANES))
+
+    def pre_slab(c, z):
+        return jnp.where(lane8 < 64, roll(R["V1"][1, 5 + z, pl.ds(RO + 4, 8), :], -4), 0.0)
+
+    wide_p = start_wide("p", 1, pre_slab)
+    coarse_setup()
     R["load"][...] = jnp.zeros(R["load"].shape, F32)
-    finish_around("f", start_around("f"), 1, store_region)
-    first_sweep(L2, lambda z: R["load"][pl.ds(pl.multiple_of(z * L2.rows, 8), L2.rows), :])
+    finish_around("f", around_f, 1, load_region(L2))
+    first_sweep(L2, load_of(L2))
     sweep(L2, 0, into(L2, 1), False, 3, 9)
     residual(L2, 1, False, 4, 8)
     values = restricted(block2, block3, 4, 4, 32)
@@ -664,9 +779,6 @@
         R["load"][pl.ds(z * L3.rows, L3.rows), :] = value
 
     gather_f.finish(store_load)
-
-    def load_of(level):
-        return lambda z: clean(level, R["load"][pl.ds(pl.multiple_of(z * level.rows, 8), level.rows), :])
 
     first_sweep(L3, load_of(L3))
     sweep(L3, 0, into(L3, 1), False)
@@ -725,10 +837,20 @@
     sweep(L3, 2, into(L3, 0), False)
     sweep(L3, 0, into(L3, 1), False)
 
-    def store_pre(i, z, row, value):
-        R["V2"][2, z + 1, pl.ds(RO + row, 4), :] = value
-
-    finish_around("p", around_p, 1, store_pre)
+    def start_region(level, slabs):
+        a, b = rows_of((LANES, LANES)), lanes_of((LANES, LANES))
+        copied = dot(jnp.concatenate(slabs, axis=0), jnp.where((a == b // 2) & (b < level.nx), 1.0, 0.0).astype(F32))
+        V = R[f"V{level.index}"]
+        for i in range(len(slabs)):
+            for phase in range(2):
+                R["spread"][0, i, pl.ds(phase, 8, stride=2), :] = copied[8 * i : 8 * i + 8]
+        for z in range(level.nz):
+            where_rows = pl.ds(RO, level.rows)
+            added = jnp.where(inside(level, z) > 0.5, R["spread"][0, z // 2, pl.ds(0, level.rows), :], 0.0)
+            V[2, z + 1, where_rows, :] = V[2, z + 1, where_rows, :] + added
+
+    finish_around("p", around_p, 1, iterate_region(2))
+    finish_wide("p", wide_p, 1, lambda i, z: R["V1"][2, z + 1, pl.ds(RO, 16), :], iterate_region(1))
     slabs = []
     count3 = L3.nz + 2
     for i in range(6):
@@ -736,27 +858,17 @@
         value = roll(value, lax.rem(2 * L3.stride - RO + 2 - 2 * gy, L3.stride), axis=0)
         value = roll(value, lax.rem(LANES + 16 - 16 * gx, LANES))
         slabs.append(value[0:8])
-    a, b = rows_of((LANES, LANES)), lanes_of((LANES, LANES))
-    copied = dot(jnp.concatenate(slabs, axis=0), jnp.where((a == b // 2) & (b < L2.nx), 1.0, 0.0).astype(F32))
-    for i in range(6):
-        for phase in range(2):
-            R["spread"][0, i, pl.ds(phase, 8, stride=2), :] = copied[8 * i : 8 * i + 8]
-    for z in range(L2.nz):
-        where_rows = pl.ds(RO, L2.rows)
-        added = jnp.where(inside(L2, z) > 0.5, R["spread"][0, z // 2, pl.ds(0, L2.rows), :], 0.0)
-        R["V2"][2, z + 1, where_rows, :] = R["V2"][2, z + 1, where_rows, :] + added
-    sweep(L2, 2, into(L2, 3), False, 2, 10)
-    sweep(L2, 3, into(L2, 0), False, 3, 9)
+    start_region(L2, slabs)
+    sweep(L2, 2, into(L2, 3), False, 1, 11)
+    sweep(L2, 3, into(L2, 0), False, 2, 10)
+    start_region(L1, [roll(R["V2"][0, 3 + i, pl.ds(RO + 2, 8), :], -30) for i in range(8)])
+    sweep(L1, 2, into(L1, 3), False, 2, 14)
+    sweep(L1, 3, into(L1, 0), False, 3, 13)
 
     def region_slab(ze):
-        return roll(R["V2"][0, 4 + ze, pl.ds(4, 24), :], -32)
-
-    spread(L1, 4, 4, 32, 24, region_slab, 0, True)
-    sweep(L1, 2, into(L1, 3))
-    exchange(L1, 3, 2)
-    sweep(L1, 3, into(L1, 0))
-    exchange(L1, 0, 3)
-    spread(L0, L1.nz, L1.ny, L1.nx, L1.stride, coarse_slab(L1, 0), 0, True)
+        return roll(R["V1"][0, 4 + ze, pl.ds(4, 24), :], -4)
+
+    spread(L0, 8, 8, 64, 24, region_slab, 0, True)
     sweep(L0, 2, into(L0, 3))
     exchange(L0, 3, 2)
 
@@ -774,8 +886,9 @@
     def body(conduct, cross, tissue, src_z, src_y, src_x):
         nz, ny, nx = tissue.shape
         sources = src_z.shape[0]
-        levels = [Level(l, nz >> l, ny >> l, nx >> l, True) for l in range(2)]
-        levels.append(Level(2, 12, 12, 96, False, True))
+        levels = [Level(0, nz, ny, nx, True)]
+        levels.append(Level(1, 16, 16, 72, False, (4, 4, 4)))
+        levels.append(Level(2, 12, 12, 96, False, (4, 4, 32)))
         levels.append(Level(3, 2 * GZ, 2 * GY, 16 * GX, False))
         levels.append(Level(4, GZ, GY, 8 * GX, False))
         scratch = {}
@@ -814,6 +927,21 @@
             vmem(f"RA{tag}", len(AROUND), height, LANES)
         scratch["asend"] = pltpu.SemaphoreType.DMA((3, len(AROUND)))
         scratch["arecv"] = pltpu.SemaphoreType.DMA((3, len(AROUND)))
+        for tag, comps in (("k", 6), ("f", 1), ("p", 1)):
+            half = (comps + 1) // 2
+            vmem(f"WA{tag}", 4, comps, 8, LANES)
+            vmem(f"WB{tag}", 2, 2, comps, 8, LANES)
+            vmem(f"WS{tag}", comps, 8, LANES)
+            vmem(f"WT{tag}", 2, half, 8, LANES)
+            vmem(f"WRA{tag}", 2, 2, comps, 8, LANES)
+            vmem(f"WRB{tag}", 2, 2, comps, 8, LANES)
+            vmem(f"WRC{tag}", 4, comps, 8, LANES)
+            vmem(f"WRS{tag}", 6, comps, 8, LANES)
+            vmem(f"WRT{tag}", 12, half, 8, LANES)
+        scratch["wsend"] = pltpu.SemaphoreType.DMA((3, len(AROUND)))
+        scratch["wrecv"] = pltpu.SemaphoreType.DMA((3, len(AROUND)))
+        vmem("strips", 3, 16, LANES)
+        vmem("KB1", 6, 8, 8, LANES)
         vmem("KB2", 6, 4, 8, LANES)
         vmem("PX", levels[0].stride, LANES)
         vmem("stage", 6 * 8 * 8, LANES)

time: 78.7 us -> 69 us (0.88)
  Pallas kernels: 77 us -> 67.3 us
    pallas_call x1, Pallas kernels: 77 us -> 67.3 us  [body(): pl.pallas_call(functools.partial(kernel, names, levels, sizes, sources),...]
where the time goes in v3:
time: 69 us; the launch traced here: 68.9 us
  Pallas kernels  67.3 us (98%)
  local copies, waits for them, and re-layouts  1.57 us (2%)
    pallas_call x1, Pallas kernels, body(): pl.pallas_call(functools.partial(kernel, names, levels, sizes, sources),...  67.3 us
    unnamed x1, local copies, waits for them, and re-layouts  1.57 us

profile of v3, /device:TPU:1, one launch (start us, length us, event | category | flops | bytes accessed | tf_op | source)
XLA Modules:
  0.0 68.9 jit_solution(11779619153014825626)
XLA Ops:
  0.0 67.3 %shard_map.64 = f32[16,16,128]{2,1,0:T(8,128)} custom-call(f32[3,16,16,128]{3,2,1,0:T(8,128)} %refs_0_.1, f32[3,16,16,128]{3,2,1,0:T(8,128)} %refs_1_.1, s32[16,16,128]{2,1,0:T(8,128)} %refs_2_.1, s32[1,2048]{1,0:T(1,128)} %bitcast.3, s32[1,2048]{1,0:T(1,128)} %bitcast.4, s32[1,2048]{1,0:T(1,128)} %bitcast.5), custom_call_target="tpu_custom_call" | custom-call | tf_op jit(solution)/shard_map/pallas_call | solution.py:968
  67.4 1.6 %copy.8 = f32[16,16,128]{2,1,0:T(8,128)} copy(f32[16,16,128]{2,1,0:T(8,128)} %shard_map.64) | data formatting | bytes 262144

commit v4 on v3

--- a/solution.py
+++ b/solution.py
@@ -59,6 +59,8 @@
     for _part, (_oy, _oz) in enumerate(((0, 0), (-1, 0), (1, 0), (0, -1), (0, 1))):
         MESSAGES.append(("p", 5 * _side + _part, (_ox, _oy, _oz)))
 AROUND = [(dx, dy, dz) for dz in (-1, 0, 1) for dy in (-1, 0, 1) for dx in (-1, 0, 1) if (dx, dy, dz) != (0, 0, 0)]
+AROUND.sort(key=lambda offset: -sum(map(abs, offset)))
+MESSAGES.sort(key=lambda message: -sum(map(abs, message[2])))
 FACES = [("z", 1, (0, 0, -1)), ("z", 0, (0, 0, 1)), ("y", 0, (0, -1, 0)), ("y", 1, (0, 1, 0)), ("p", 0, (-1, 0, 0)), ("p", 1, (1, 0, 0))]
 
 

time: 69 us -> 69 us (level)
  no operation moved by 1% of the time
where the time goes in v4:
time: 69 us; the launch traced here: 68.9 us
  Pallas kernels  67.3 us (98%)
  local copies, waits for them, and re-layouts  1.57 us (2%)
    pallas_call x1, Pallas kernels, body(): pl.pallas_call(functools.partial(kernel, names, levels, sizes, sources),...  67.3 us
    unnamed x1, local copies, waits for them, and re-layouts  1.57 us

profile of v4, /device:TPU:1, one launch (start us, length us, event | category | flops | bytes accessed | tf_op | source)
XLA Modules:
  0.0 68.9 jit_solution(5620917611282183525)
XLA Ops:
  0.0 67.3 %shard_map.64 = f32[16,16,128]{2,1,0:T(8,128)} custom-call(f32[3,16,16,128]{3,2,1,0:T(8,128)} %refs_0_.1, f32[3,16,16,128]{3,2,1,0:T(8,128)} %refs_1_.1, s32[16,16,128]{2,1,0:T(8,128)} %refs_2_.1, s32[1,2048]{1,0:T(1,128)} %bitcast.3, s32[1,2048]{1,0:T(1,128)} %bitcast.4, s32[1,2048]{1,0:T(1,128)} %bitcast.5), custom_call_target="tpu_custom_call" | custom-call | tf_op jit(solution)/shard_map/pallas_call | solution.py:970
  67.3 1.6 %copy.8 = f32[16,16,128]{2,1,0:T(8,128)} copy(f32[16,16,128]{2,1,0:T(8,128)} %shard_map.64) | data formatting | bytes 262144

commit v5 on v4

--- a/solution.py
+++ b/solution.py
@@ -751,12 +751,6 @@
 
     block2_tile(R["TAf"], 1, values)
     around_f = start_around("f")
-    lane8 = lanes_of((8, LANES))
-
-    def pre_slab(c, z):
-        return jnp.where(lane8 < 64, roll(R["V1"][1, 5 + z, pl.ds(RO + 4, 8), :], -4), 0.0)
-
-    wide_p = start_wide("p", 1, pre_slab)
     coarse_setup()
     R["load"][...] = jnp.zeros(R["load"].shape, F32)
     finish_around("f", around_f, 1, load_region(L2))
@@ -767,6 +761,8 @@
 
     gather_f = Gather("f", 1)
     gather_f.phase_x(own_tile(values, 1, 8))
+    gather_f.phase_y()
+    gather_f.phase_z()
     tile_lane = lanes_of((8, LANES))
     total = jnp.zeros((8, LANES), F32)
     for z in range(4):
@@ -774,8 +770,12 @@
         total = jnp.where((tile_lane >= 32 * z) & (tile_lane < 32 * z + 32), piece, total)
     R["TAp"][0:4, :] = total[0:4]
     around_p = start_around("p")
-    gather_f.phase_y()
-    gather_f.phase_z()
+    lane8 = lanes_of((8, LANES))
+
+    def pre_slab(c, z):
+        return jnp.where(lane8 < 64, roll(R["V1"][1, 5 + z, pl.ds(RO + 4, 8), :], -4), 0.0)
+
+    wide_p = start_wide("p", 1, pre_slab)
 
     def store_load(i, z, value):
         R["load"][pl.ds(z * L3.rows, L3.rows), :] = value
@@ -852,7 +852,6 @@
             V[2, z + 1, where_rows, :] = V[2, z + 1, where_rows, :] + added
 
     finish_around("p", around_p, 1, iterate_region(2))
-    finish_wide("p", wide_p, 1, lambda i, z: R["V1"][2, z + 1, pl.ds(RO, 16), :], iterate_region(1))
     slabs = []
     count3 = L3.nz + 2
     for i in range(6):
@@ -863,6 +862,7 @@
     start_region(L2, slabs)
     sweep(L2, 2, into(L2, 3), False, 1, 11)
     sweep(L2, 3, into(L2, 0), False, 2, 10)
+    finish_wide("p", wide_p, 1, lambda i, z: R["V1"][2, z + 1, pl.ds(RO, 16), :], iterate_region(1))
     start_region(L1, [roll(R["V2"][0, 3 + i, pl.ds(RO + 2, 8), :], -30) for i in range(8)])
     sweep(L1, 2, into(L1, 3), False, 2, 14)
     sweep(L1, 3, into(L1, 0), False, 3, 13)

time: 69 us -> 68.9 us (level)
  no operation moved by 1% of the time
where the time goes in v5:
time: 68.9 us; the launch traced here: 68.7 us
  Pallas kernels  67.2 us (98%)
  local copies, waits for them, and re-layouts  1.57 us (2%)
    pallas_call x1, Pallas kernels, body(): pl.pallas_call(functools.partial(kernel, names, levels, sizes, sources),...  67.2 us
    unnamed x1, local copies, waits for them, and re-layouts  1.57 us

profile of v5, /device:TPU:1, one launch (start us, length us, event | category | flops | bytes accessed | tf_op | source)
XLA Modules:
  0.0 68.7 jit_solution(6422820870101159789)
XLA Ops:
  0.0 67.2 %shard_map.64 = f32[16,16,128]{2,1,0:T(8,128)} custom-call(f32[3,16,16,128]{3,2,1,0:T(8,128)} %refs_0_.1, f32[3,16,16,128]{3,2,1,0:T(8,128)} %refs_1_.1, s32[16,16,128]{2,1,0:T(8,128)} %refs_2_.1, s32[1,2048]{1,0:T(1,128)} %bitcast.3, s32[1,2048]{1,0:T(1,128)} %bitcast.4, s32[1,2048]{1,0:T(1,128)} %bitcast.5), custom_call_target="tpu_custom_call" | custom-call | tf_op jit(solution)/shard_map/pallas_call | solution.py:970
  67.2 1.6 %copy.8 = f32[16,16,128]{2,1,0:T(8,128)} copy(f32[16,16,128]{2,1,0:T(8,128)} %shard_map.64) | data formatting | bytes 262144
